TPU v7x, 512 devices: a whole 4x8x8 slice. The times are simulated.
512 devices in a mesh: interval: 8 (over y), seq: 8 (over x, core), head: 8 (over z).
Axes of the slice: x: 4, y: 8, z: 8, core: 2. Of those that a mesh axis runs over, the one named last changes fastest.
Arguments:
- hidden_in: bfloat16 [8, 2048, 1536], P('interval', 'seq'), may hold values from -6 to 6
- ctx_grad: bfloat16 [8, 2048, 1536], P('interval', 'seq', 'head'), may hold values from -6 to 6
- w_query: bfloat16 [1536, 1536], P('head'), may hold values from -0.15625 to 0.15625
- w_key: bfloat16 [1536, 1536], P('head'), may hold values from -0.15625 to 0.15625
- w_value: bfloat16 [1536, 1536], P('head'), may hold values from -0.15625 to 0.15625
- w_junction: bfloat16 [1536, 128], replicated, may hold values from -0.15625 to 0.15625
- donor_pos: int32 [8, 8, 8, 64], P('interval', 'seq', None, 'head'), may hold values from 0 to 255
- acceptor_pos: int32 [8, 8, 8, 64], P('interval', 'seq', None, 'head'), may hold values from 0 to 255
- junction_counts: int32 [8, 8, 8], P('interval', 'seq'), may hold values from 16 to 64, as said below
- pred_grad: float32 [8, 8, 8, 64], P('interval', 'seq', None, 'head'), may hold values from -6 to 6
Outputs:
- grad_input: bfloat16 [8, 2048, 1536], P('interval', 'seq', 'head')
- grad_query: bfloat16 [1536, 1536], P('head')
- grad_key: bfloat16 [1536, 1536], P('head')
- grad_value: bfloat16 [1536, 1536], P('head')
Inputs may be any that keep to these rules, and one draw needn't show every extreme that they name: `junction_counts`: slots at or past a bucket's count are empty. In each interval one acceptor shard, drawn from the seed, has 64 live slots from every donor shard; every other bucket has 16 to 32.
All inputs are finite; a program needn't handle non-finite values.
Results may differ from a plain program's by a relative error of at most 0.022.
Values may be sent and summed in bfloat16 or wider, within the bound.
No kernel may reach another device: no remote copies, remote signals or barrier semaphores. Data moves between devices by JAX's collectives and lax.ppermute only.
A program may use at most 64 MiB of HBM per device.

v0:
```python
import jax
import jax.numpy as jnp
from jax import lax
from jax.sharding import PartitionSpec as P

HD = 192
PJ = 128


def on_device(
    hidden_in,
    ctx_grad,
    w_query,
    w_key,
    w_value,
    w_junction,
    donor_pos,
    acceptor_pos,
    junction_counts,
    pred_grad,
):
    hidden = hidden_in[0]
    local_len = hidden.shape[0]
    shard_count = lax.axis_size("seq")
    total_len = local_len * shard_count
    heads_dev = w_query.shape[0] // HD
    softmax_scale = HD ** (-0.5)
    pair_scale = PJ ** (-0.5)
    queries = jnp.einsum("td,cd->tc", hidden, w_query, preferred_element_type=jnp.float32).astype(
        jnp.bfloat16
    )
    key_rows = jnp.einsum("td,cd->tc", hidden, w_key, preferred_element_type=jnp.float32).astype(
        jnp.bfloat16
    )
    value_rows = jnp.einsum(
        "td,cd->tc", hidden, w_value, preferred_element_type=jnp.float32
    ).astype(jnp.bfloat16)
    features = jnp.dot(hidden, w_junction, preferred_element_type=jnp.float32).astype(jnp.bfloat16)
    all_keys, all_values, all_features = (
        lax.all_gather(key_rows, "seq", axis=0, tiled=True),
        lax.all_gather(value_rows, "seq", axis=0, tiled=True),
        lax.all_gather(features, "seq", axis=0, tiled=True),
    )
    query_heads = queries.reshape(local_len, heads_dev, HD)
    grad_heads = ctx_grad[0].reshape(local_len, heads_dev, HD)
    key_heads = all_keys.reshape(total_len, heads_dev, HD)
    value_heads = all_values.reshape(total_len, heads_dev, HD)
    scores = (
        jnp.einsum("qhd,khd->hqk", query_heads, key_heads, preferred_element_type=jnp.float32)
        * softmax_scale
    )
    row_max = jnp.max(scores, axis=-1, keepdims=True)
    expd = jnp.exp(scores - row_max)
    probs = expd / jnp.sum(expd, axis=-1, keepdims=True)
    dprobs = jnp.einsum("qhd,khd->hqk", grad_heads, value_heads, preferred_element_type=jnp.float32)
    row_delta = jnp.sum(probs * dprobs, axis=-1, keepdims=True)
    dscores = probs * (dprobs - row_delta)
    probs_b = probs.astype(jnp.bfloat16)
    dscores_b = dscores.astype(jnp.bfloat16)
    query_grad = (
        (
            jnp.einsum("hqk,khd->qhd", dscores_b, key_heads, preferred_element_type=jnp.float32)
            * softmax_scale
        )
        .astype(jnp.bfloat16)
        .reshape(local_len, heads_dev * HD)
    )
    key_term = (
        jnp.einsum("hqk,qhd->khd", dscores_b, query_heads, preferred_element_type=jnp.float32)
        * softmax_scale
    ).reshape(total_len, heads_dev * HD)
    value_term = jnp.einsum(
        "hqk,qhd->khd", probs_b, grad_heads, preferred_element_type=jnp.float32
    ).reshape(total_len, heads_dev * HD)
    key_sum, value_sum = (
        lax.psum_scatter(
            key_term.astype(jnp.bfloat16), "seq", scatter_dimension=0, tiled=True
        ).astype(jnp.float32),
        lax.psum_scatter(
            value_term.astype(jnp.bfloat16), "seq", scatter_dimension=0, tiled=True
        ).astype(jnp.float32),
    )
    key_grad = key_sum.astype(jnp.bfloat16)
    value_grad = value_sum.astype(jnp.bfloat16)
    donor_idx = donor_pos[0, 0]
    accept_idx = acceptor_pos[0, 0]
    slot_dev = donor_idx.shape[1]
    slot_ids = lax.axis_index("head") * slot_dev + jnp.arange(slot_dev, dtype=jnp.int32)
    live_slots = slot_ids[None, :] < junction_counts[0, 0][:, None]
    donor_feat = features[donor_idx].astype(jnp.float32)
    accept_glob = jnp.arange(shard_count, dtype=jnp.int32)[:, None] * local_len + accept_idx
    accept_rows = all_features[accept_glob]
    accept_feat = accept_rows.astype(jnp.float32)
    pair_score = jnp.sum(donor_feat * accept_feat, axis=-1) * pair_scale
    slot_grad = (
        jnp.where(live_slots, pred_grad[0, 0] * jax.nn.sigmoid(pair_score), 0.0) * pair_scale
    )
    donor_term = slot_grad[..., None] * accept_feat
    accept_term = slot_grad[..., None] * donor_feat
    pair_width = features.shape[1]
    grad_feat = (
        jnp.zeros((local_len, pair_width), jnp.float32)
        .at[donor_idx.reshape(-1)]
        .add(donor_term.reshape(-1, pair_width))
    )
    spread_term = (
        jnp.zeros((total_len, pair_width), jnp.float32)
        .at[accept_glob.reshape(-1)]
        .add(accept_term.reshape(-1, pair_width))
    )
    grad_feat = grad_feat + lax.psum_scatter(
        spread_term.astype(jnp.bfloat16), "seq", scatter_dimension=0, tiled=True
    ).astype(jnp.float32)
    grad_feat_b = grad_feat.astype(jnp.bfloat16)
    input_term = jnp.einsum("tc,cd->td", query_grad, w_query, preferred_element_type=jnp.float32)
    input_term = input_term + jnp.einsum(
        "tc,cd->td", key_grad, w_key, preferred_element_type=jnp.float32
    )
    input_term = input_term + jnp.einsum(
        "tc,cd->td", value_grad, w_value, preferred_element_type=jnp.float32
    )
    input_term = input_term + jnp.einsum(
        "tp,dp->td", grad_feat_b, w_junction, preferred_element_type=jnp.float32
    )
    grad_input = lax.psum_scatter(
        input_term.astype(jnp.bfloat16), "head", scatter_dimension=1, tiled=True
    )
    key_wterm = jnp.einsum("tc,td->cd", key_grad, hidden, preferred_element_type=jnp.float32)
    value_wterm = jnp.einsum("tc,td->cd", value_grad, hidden, preferred_element_type=jnp.float32)
    query_wterm = jnp.einsum("tc,td->cd", query_grad, hidden, preferred_element_type=jnp.float32)
    query_wsum, key_wsum, value_wsum = lax.psum(
        (query_wterm, key_wterm, value_wterm), ("interval", "seq")
    )
    return (
        grad_input[None],
        query_wsum.astype(jnp.bfloat16),
        key_wsum.astype(jnp.bfloat16),
        value_wsum.astype(jnp.bfloat16),
    )


def solution(mesh):
    placed = (
        P("interval", "seq", None),
        P("interval", "seq", "head"),
        P("head", None),
        P("head", None),
        P("head", None),
        P(),
        P("interval", "seq", None, "head"),
        P("interval", "seq", None, "head"),
        P("interval", "seq", None),
        P("interval", "seq", None, "head"),
    )
    return jax.shard_map(
        on_device,
        mesh=mesh,
        in_specs=placed,
        out_specs=(P("interval", "seq", "head"), P("head", None), P("head", None), P("head", None)),
        check_vma=False,
    )
```

profile of v0, /device:TPU:64, one launch (start us, length us, event | category | flops | bytes accessed | tf_op | source)
XLA Modules:
  0.0 447.5 jit_solution(17675293737374444175)
XLA Ops:
  7.2 0.8 squeeze.15
  8.1 0.8 compare_select_fusion
  9.0 0.7 compare_select_fusion.1
  9.8 1.3 convolution_convert_fusion.4
  11.1 13.6 %all_gather.11 = bf16[2048,128]{1,0:T(8,128)(2,1)S(1)} all-gather(bf16[256,128]{1,0:T(8,128)(2,1)S(1)} %convolution_convert_fusion.4), channel_id=1, replica_groups=mesh['interval'=8,'seq'=8,'head'=8] {'seq'}, dimensions={0}, use_global_device_ids=true | all-gather | bytes 589824 | tf_op jit(solution)/shard_map/all_gather | solution.py:42
  24.7 0.6 gather_fusion
  25.4 0.8 squeeze.16
  26.3 0.7 lt.67
  27.1 0.6 gather_fusion.1
  27.9 1.1 scatter_custom_fusion
  29.1 0.8 convert_element_type.105
  30.4 13.4 %all_gather.9 = bf16[2048,192]{0,1:T(8,128)(2,1)S(1)} all-gather(bf16[256,192]{0,1:T(8,128)(2,1)S(1)} %convolution_convert_fusion.3), channel_id=1, replica_groups=mesh['interval'=8,'seq'=8,'head'=8] {'seq'}, dimensions={0}, use_global_device_ids=true | all-gather | bytes 884736 | tf_op jit(solution)/shard_map/all_gather | solution.py:40
  44.6 14.2 %all_gather.10 = bf16[2048,192]{1,0:T(8,128)(2,1)S(1)} all-gather(bf16[256,192]{1,0:T(8,128)(2,1)S(1)} %convolution_convert_fusion.1), channel_id=1, replica_groups=mesh['interval'=8,'seq'=8,'head'=8] {'seq'}, dimensions={0}, use_global_device_ids=true | all-gather | bytes 884736 | tf_op jit(solution)/shard_map/all_gather | solution.py:41
  58.8 0.5 fusion.31
  59.8 0.7 multiply_reduce_fusion
  60.5 0.6 multiply_convert_fusion
  61.1 1.0 copy-done.1
  62.1 1.3 fusion.2
  63.5 2.4 convolution_convert_fusion
  66.1 2.0 fusion.6
  68.1 0.5 fusion.32
  68.6 1.5 reduce-scatter.9.cloned.1.call-done
  70.1 0.8 convert_element_type.106
  70.9 1.1 scatter_custom_fusion.1
  72.0 37.1 %reduce-scatter.5.cloned.1.call-done = bf16[256,192]{0,1:T(8,128)(2,1)} async-done(((bf16[2048,192]{0,1:T(8,128)(2,1)}), bf16[256,192]{0,1:T(8,128)(2,1)}) %reduce-scatter.5.cloned.1.call-update) | async-done | bytes 98320 | tf_op jit(solution)/shard_map/reduce_scatter | solution.py:76
  109.1 2.7 convolution_add_fusion.2
  111.8 35.7 %reduce-scatter.7.cloned.1.call-done = bf16[256,192]{0,1:T(8,128)(2,1)} async-done(((bf16[2048,192]{0,1:T(8,128)(2,1)}), bf16[256,192]{0,1:T(8,128)(2,1)}) %reduce-scatter.7.cloned.1.call-update) | async-done | bytes 98320 | tf_op jit(solution)/shard_map/reduce_scatter | solution.py:79
  147.5 1.9 convolution_add_fusion.1
  149.5 1.3 fusion
  151.1 0.5 copy-done.8
  152.0 1.3 fusion.8
  153.3 287.6 %all-reduce.2 = (bf16[192,1536]{1,0:T(8,128)(2,1)}, bf16[192,1536]{1,0:T(8,128)(2,1)}, bf16[192,1536]{1,0:T(8,128)(2,1)}) all-reduce(f32[192,1536]{1,0:T(8,128)S(1)} %fusion.12, f32[192,1536]{1,0:T(8,128)S(1)} %fusion.10, f32[192,1536]{1,0:T(8,128)} %fusion.8), channel_id=1, replica_groups=mesh['interval'=8,'seq'=8,'head'=8] {'interval','seq'}, use_global_device_ids=true, to_apply=%region_10.11 | all-reduce | flops 884736 | bytes 5308416 | tf_op jit(solution)/shard_map/psum | solution.py:131
  (53 shorter events, 3.3 us)
Async XLA Ops:
  7.2 2.6 copy-start
  7.2 62.9 %reduce-scatter.9.cloned.1.call-start = ((), (), s32[]{:S(2)}) async-start(), calls=%async_computation.6 | async-start | bytes 589824 | tf_op jit(solution)/shard_map/reduce_scatter | solution.py:111
  11.1 18.9 %copy-start.4 = (bf16[192,1536]{1,0:T(8,128)(2,1)S(1)}, bf16[192,1536]{1,0:T(8,128)(2,1)}, u32[]{:S(2)}) copy-start(bf16[192,1536]{1,0:T(8,128)(2,1)} %param.13) | copy-start | bytes 1769476
  29.1 14.7 %copy-start.3 = (bf16[192,1536]{1,0:T(8,128)(2,1)S(1)}, bf16[192,1536]{1,0:T(8,128)(2,1)}, u32[]{:S(2)}) copy-start(bf16[192,1536]{1,0:T(8,128)(2,1)} %param.12) | copy-start | bytes 1769476
  29.9 14.3 %copy-start.6 = (bf16[192,1536]{1,0:T(8,128)(2,1)S(1)}, bf16[192,1536]{1,0:T(8,128)(2,1)}, u32[]{:S(2)}) copy-start(bf16[192,1536]{1,0:T(8,128)(2,1)} %param.14) | copy-start | bytes 1769476
  29.9 79.1 %reduce-scatter.5.cloned.1.call-start = ((), (), s32[]{:S(2)}) async-start(), calls=%async_computation.4 | async-start | bytes 884736 | tf_op jit(solution)/shard_map/reduce_scatter | solution.py:76
  43.8 15.0 %copy-start.2 = (bf16[2048,192]{0,1:T(8,128)(2,1)}, bf16[2048,192]{0,1:T(8,128)(2,1)S(1)}, u32[]{:S(2)}) copy-start(bf16[2048,192]{0,1:T(8,128)(2,1)S(1)} %all_gather.9) | copy-start | bytes 2359300
  58.8 1.0 copy-start.11
  61.1 1.0 copy-start.1
  63.5 2.6 copy-start.10
  63.5 84.0 %reduce-scatter.7.cloned.1.call-start = ((), (), s32[]{:S(2)}) async-start(), calls=%async_computation.5 | async-start | bytes 884736 | tf_op jit(solution)/shard_map/reduce_scatter | solution.py:79
  66.0 375.0 %reduce-scatter.11.cloned.1.call-start = ((), (), s32[]{:S(2)}) async-start(), calls=%async_computation.7 | async-start | bytes 884736 | tf_op jit(solution)/shard_map/reduce_scatter | solution.py:125
  68.6 79.0 %copy-start.7 = (bf16[192,1536]{1,0:T(8,128)(2,1)S(1)}, bf16[192,1536]{1,0:T(8,128)(2,1)}, u32[]{:S(2)}) copy-start(bf16[192,1536]{1,0:T(8,128)(2,1)} %param.14) | copy-start | bytes 1769476
  111.8 37.6 %copy-start.5 = (bf16[1536,128]{1,0:T(8,128)(2,1)S(1)}, bf16[1536,128]{1,0:T(8,128)(2,1)}, u32[]{:S(2)}) copy-start(bf16[1536,128]{1,0:T(8,128)(2,1)} %param.15) | copy-start | bytes 1179652
  150.7 0.9 copy-start.8
  150.8 1.2 copy-start.9
Sparse Core Ops, SparseCore 0:
  30.1 39.9 reduce-scatter.8
  73.1 35.9 reduce-scatter.4
  111.9 35.5 reduce-scatter.6
  151.0 39.1 reduce-scatter.10
where the time goes:
time: 448 us; the launch traced here: 447 us
  blocking collectives  329 us (73%)
  waiting for transfers between devices  74.4 us (17%)
  matrix products  17.9 us (4%)
  between operations  14 us (3%)
  other arithmetic  6.55 us (1%)
  local copies, waits for them, and re-layouts  5.71 us (1%)
    psum x1, blocking collectives, on_device(): lax.psum((query_wterm, key_wterm, value_wterm), ('interval', 'seq'))  288 us
    reduce_scatter x1, waiting for transfers between devices, on_device(): lax.psum_scatter(key_term.astype(jnp.bfloat16), 'seq', scatter_dimension=...  37.1 us
    reduce_scatter x1, waiting for transfers between devices, on_device(): lax.psum_scatter(value_term.astype(jnp.bfloat16), 'seq', scatter_dimensio...  35.7 us
    all_gather x1, blocking collectives, on_device(): lax.all_gather(value_rows, 'seq', axis=0, tiled=True)  14.2 us
    all_gather x1, blocking collectives, on_device(): lax.all_gather(features, 'seq', axis=0, tiled=True)  13.6 us
    all_gather x1, blocking collectives, on_device(): lax.all_gather(key_rows, 'seq', axis=0, tiled=True)  13.4 us
  transfers between devices with their start and end apart: 4, of which 3 were waited for; matrix products, arithmetic and copies ran while one was open for 4% of the time, Pallas kernels for 0%

commit v1 on v0

--- a/solution.py
+++ b/solution.py
@@ -129,7 +129,7 @@
     value_wterm = jnp.einsum("tc,td->cd", value_grad, hidden, preferred_element_type=jnp.float32)
     query_wterm = jnp.einsum("tc,td->cd", query_grad, hidden, preferred_element_type=jnp.float32)
     query_wsum, key_wsum, value_wsum = lax.psum(
-        (query_wterm, key_wterm, value_wterm), ("interval", "seq")
+        lax.psum((query_wterm, key_wterm, value_wterm), "seq"), "interval"
     )
     return (
         grad_input[None],

time: 448 us -> 328 us (0.73)
  the two profiles are of different devices: /device:TPU:64 before, /device:TPU:16 now
where the time goes in v1:
time: 328 us; the launch traced here: 327 us
  waiting for transfers between devices  160 us (49%)
  blocking collectives  119 us (36%)
  matrix products  20.5 us (6%)
  between operations  14.1 us (4%)
  other arithmetic  7.82 us (2%)
  local copies, waits for them, and re-layouts  5.88 us (2%)
    psum x1, blocking collectives, on_device(): lax.psum(lax.psum((query_wterm, key_wterm, value_wterm), 'seq'), 'interval')  76.9 us
    psum x1, waiting for transfers between devices, on_device(): lax.psum((query_wterm, key_wterm, value_wterm), 'seq')  76.4 us
    reduce_scatter x1, waiting for transfers between devices, on_device(): lax.psum_scatter(value_term.astype(jnp.bfloat16), 'seq', scatter_dimensio...  36.5 us
    reduce_scatter x1, waiting for transfers between devices, on_device(): lax.psum_scatter(spread_term.astype(jnp.bfloat16), 'seq', scatter_dimensi...  34.2 us
    all_gather x1, blocking collectives, on_device(): lax.all_gather(features, 'seq', axis=0, tiled=True)  14.2 us
    all_gather x1, blocking collectives, on_device(): lax.all_gather(value_rows, 'seq', axis=0, tiled=True)  13.7 us
    all_gather x1, blocking collectives, on_device(): lax.all_gather(key_rows, 'seq', axis=0, tiled=True)  13.7 us
    reduce_scatter x1, waiting for transfers between devices, on_device(): lax.psum_scatter(key_term.astype(jnp.bfloat16), 'seq', scatter_dimension=...  12.9 us
  transfers between devices with their start and end apart: 5, of which 4 were waited for; matrix products, arithmetic and copies ran while one was open for 8% of the time, Pallas kernels for 0%

profile of v1, /device:TPU:16, one launch (start us, length us, event | category | flops | bytes accessed | tf_op | source)
XLA Modules:
  0.0 327.2 jit_solution(11649827562936686372)
XLA Ops:
  7.2 1.1 copy-done
  8.3 1.5 convolution_convert_fusion.3
  9.8 13.7 %all_gather.9 = bf16[2048,192]{0,1:T(8,128)(2,1)S(1)} all-gather(bf16[256,192]{0,1:T(8,128)(2,1)S(1)} %convolution_convert_fusion.3), channel_id=1, replica_groups=mesh['interval'=8,'seq'=8,'head'=8] {'seq'}, dimensions={0}, use_global_device_ids=true | all-gather | bytes 884736 | tf_op jit(solution)/shard_map/all_gather | solution.py:40
  24.3 13.7 %all_gather.10 = bf16[2048,192]{1,0:T(8,128)(2,1)S(1)} all-gather(bf16[256,192]{1,0:T(8,128)(2,1)S(1)} %convolution_convert_fusion.1), channel_id=1, replica_groups=mesh['interval'=8,'seq'=8,'head'=8] {'seq'}, dimensions={0}, use_global_device_ids=true | all-gather | bytes 884736 | tf_op jit(solution)/shard_map/all_gather | solution.py:41
  38.1 0.5 fusion.31
  39.1 0.7 multiply_reduce_fusion
  39.8 0.6 multiply_convert_fusion
  40.4 1.0 copy-done.1
  41.4 1.3 fusion.2
  42.8 2.4 convolution_convert_fusion
  46.2 1.4 convolution_convert_fusion.4
  47.5 0.6 gather_fusion
  48.2 14.2 %all_gather.11 = bf16[2048,128]{1,0:T(8,128)(2,1)} all-gather(bf16[256,128]{1,0:T(8,128)(2,1)S(1)} %convolution_convert_fusion.4), channel_id=1, replica_groups=mesh['interval'=8,'seq'=8,'head'=8] {'seq'}, dimensions={0}, use_global_device_ids=true | all-gather | bytes 589824 | tf_op jit(solution)/shard_map/all_gather | solution.py:42
  62.4 1.7 gather_fusion.1
  64.2 1.9 scatter_custom_fusion
  66.2 2.1 convert_element_type.105
  68.9 0.6 copy-done.8
  69.5 1.3 fusion.12
  70.8 12.9 %reduce-scatter.5.cloned.1.call-done = bf16[256,192]{0,1:T(8,128)(2,1)} async-done(((bf16[2048,192]{0,1:T(8,128)(2,1)}), bf16[256,192]{0,1:T(8,128)(2,1)}) %reduce-scatter.5.cloned.1.call-update) | async-done | bytes 98320 | tf_op jit(solution)/shard_map/reduce_scatter | solution.py:76
  83.7 2.3 fusion.10
  86.0 36.5 %reduce-scatter.7.cloned.1.call-done = bf16[256,192]{0,1:T(8,128)(2,1)} async-done(((bf16[2048,192]{0,1:T(8,128)(2,1)}), bf16[256,192]{0,1:T(8,128)(2,1)}) %reduce-scatter.7.cloned.1.call-update) | async-done | bytes 98320 | tf_op jit(solution)/shard_map/reduce_scatter | solution.py:79
  122.5 2.2 fusion.8
  124.9 0.5 fusion.28
  125.4 1.3 fusion.32
  126.7 34.2 %reduce-scatter.9.cloned.1.call-done = bf16[256,128]{1,0:T(8,128)(2,1)} async-done(((bf16[2048,128]{1,0:T(8,128)(2,1)}), bf16[256,128]{1,0:T(8,128)(2,1)}) %reduce-scatter.9.cloned.1.call-update) | async-done | bytes 65552 | tf_op jit(solution)/shard_map/reduce_scatter | solution.py:111
  161.0 0.8 convert_element_type.106
  161.8 1.2 scatter_custom_fusion.1
  163.0 1.3 convolution_add_fusion.2
  164.4 1.6 convolution_add_fusion.1
  166.0 1.2 fusion
  167.3 76.4 %all-reduce.5.cloned.1.call-done = (f32[192,1536]{1,0:T(8,128)}, f32[192,1536]{1,0:T(8,128)}, f32[192,1536]{1,0:T(8,128)}) async-done(((f32[192,1536]{1,0:T(8,128)}, f32[192,1536]{1,0:T(8,128)}, f32[192,1536]{1,0:T(8,128)}), (f32[192,1536]{1,0:T(8,128)}, f32[192,1536]{1,0:T(8,128)}, f32[192,1536]{1,0:T(8,128)})) %all-reduce.5.cloned.1.call-update) | async-done | bytes 3538960 | tf_op jit(solution)/shard_map/psum | solution.py:132
  243.7 76.9 %all-reduce.6 = (bf16[192,1536]{1,0:T(8,128)(2,1)}, bf16[192,1536]{1,0:T(8,128)(2,1)}, bf16[192,1536]{1,0:T(8,128)(2,1)}) all-reduce(f32[192,1536]{1,0:T(8,128)} %get-tuple-element.4, f32[192,1536]{1,0:T(8,128)} %get-tuple-element.5, f32[192,1536]{1,0:T(8,128)} %get-tuple-element.6), channel_id=1, replica_groups=mesh['interval'=8,'seq'=8,'head'=8] {'interval'}, use_global_device_ids=true, to_apply=%region_11.12 | all-reduce | flops 884736 | bytes 5308416 | tf_op jit(solution)/shard_map/psum | solution.py:131
  (64 shorter events, 3.1 us)
Async XLA Ops:
  7.2 1.1 copy-start
  7.2 16.3 %copy-start.5 = (bf16[192,1536]{1,0:T(8,128)(2,1)S(1)}, bf16[192,1536]{1,0:T(8,128)(2,1)}, u32[]{:S(2)}) copy-start(bf16[192,1536]{1,0:T(8,128)(2,1)} %param.12) | copy-start | bytes 1769476
  7.2 16.7 %copy-start.9 = (bf16[192,1536]{1,0:T(8,128)(2,1)S(1)}, bf16[192,1536]{1,0:T(8,128)(2,1)}, u32[]{:S(2)}) copy-start(bf16[192,1536]{1,0:T(8,128)(2,1)} %param.14) | copy-start | bytes 1769476
  7.2 76.5 %reduce-scatter.5.cloned.1.call-start = ((), (), s32[]{:S(2)}) async-start(), calls=%async_computation.4 | async-start | bytes 884736 | tf_op jit(solution)/shard_map/reduce_scatter | solution.py:76
  23.5 14.6 %copy-start.3 = (bf16[2048,192]{0,1:T(8,128)(2,1)}, bf16[2048,192]{0,1:T(8,128)(2,1)S(1)}, u32[]{:S(2)}) copy-start(bf16[2048,192]{0,1:T(8,128)(2,1)S(1)} %all_gather.9) | copy-start | bytes 2359300
  38.1 1.0 copy-start.15
  40.4 1.0 copy-start.1
  42.7 2.8 copy-start.10
  42.7 2.8 copy-start.11
  42.7 2.9 copy-start.13
  42.7 3.3 copy-start.14
  42.8 79.7 %reduce-scatter.7.cloned.1.call-start = ((), (), s32[]{:S(2)}) async-start(), calls=%async_computation.5 | async-start | bytes 884736 | tf_op jit(solution)/shard_map/reduce_scatter | solution.py:79
  45.3 115.7 %reduce-scatter.9.cloned.1.call-start = ((), (), s32[]{:S(2)}) async-start(), calls=%async_computation.6 | async-start | bytes 589824 | tf_op jit(solution)/shard_map/reduce_scatter | solution.py:111
  47.5 20.8 %copy-start.2 = (bf16[256,2048]{1,0:T(8,128)(2,1)S(1)}, bf16[256,2048]{1,0:T(8,128)(2,1)}, u32[]{:S(2)}) copy-start(bf16[256,2048]{1,0:T(8,128)(2,1)} %copy-done.1) | copy-start | bytes 3145732
  47.5 20.8 %copy-start.4 = (bf16[2048,192]{0,1:T(8,128)(2,1)S(1)}, bf16[2048,192]{0,1:T(8,128)(2,1)}, u32[]{:S(2)}) copy-start(bf16[2048,192]{0,1:T(8,128)(2,1)} %copy-done.3) | copy-start | bytes 2359300
  64.2 4.6 %copy-start.12 = (f32[64]{0:T(128)}, f32[64]{0:T(128)S(1)}, u32[]{:S(2)}) copy-start(f32[64]{0:T(128)S(1)} %fusion.29) | copy-start | bytes 772
  68.3 175.5 %all-reduce.5.cloned.1.call-start = ((), (), s32[]{:S(2)}) async-start(), calls=%async_computation.8 | async-start | bytes 7077888 | tf_op jit(solution)/shard_map/psum | solution.py:132
  68.8 0.6 copy-start.8
  124.7 38.3 %copy-start.6 = (bf16[192,1536]{1,0:T(8,128)(2,1)S(1)}, bf16[192,1536]{1,0:T(8,128)(2,1)}, u32[]{:S(2)}) copy-start(bf16[192,1536]{1,0:T(8,128)(2,1)} %param.13) | copy-start | bytes 1769476
  124.7 195.9 %reduce-scatter.11.cloned.1.call-start = ((), (), s32[]{:S(2)}) async-start(), calls=%async_computation.7 | async-start | bytes 884736 | tf_op jit(solution)/shard_map/reduce_scatter | solution.py:125
  164.4 1.6 copy-start.7
Sparse Core Ops, SparseCore 0:
  42.8 40.8 reduce-scatter.4
  86.8 35.6 reduce-scatter.6
  125.9 35.0 reduce-scatter.8
  163.6 80.1 all-reduce.4
  247.0 41.3 reduce-scatter.10
